TPU v7x, 128 devices: a whole 4x4x4 slice. The times are simulated.
128 devices in a mesh: dp: 8 (over x_lo, y), expert: 16 (over x_hi, z, core).
Axes of the slice: x: 4 (x_hi: 2, x_lo: 2; x = x_hi * 2 + x_lo), y: 4, z: 4, core: 2. Of those that a mesh axis runs over, the one named last changes fastest.
Arguments:
- tokens: bfloat16 [65536, 2048], P(('dp', 'expert')), may hold values from -6 to 6
- probe: bfloat16 [65536, 2048], P(('dp', 'expert')), may hold values from -20 to 20
- domain: int32 [65536], P(('dp', 'expert')), may hold values from 0 to 21
- mix: float32 [22], replicated, may hold values from 0.5 to 2
- router: bfloat16 [2048, 32], replicated, may hold values from -0.125 to 0.125
- picks: int32 [128, 32, 40], P(('dp', 'expert')), may hold values from 0 to 511, as said below
- w_gate: bfloat16 [2048, 32, 768], P(None, 'expert'), may hold values from -0.125 to 0.125
- w_up: bfloat16 [2048, 32, 768], P(None, 'expert'), may hold values from -0.125 to 0.125
- w_down: bfloat16 [2048, 32, 768], P(None, 'expert'), may hold values from -0.21875 to 0.21875
Outputs:
- domain_loss: float32 [22], replicated
- router_grad: float32 [2048, 32], replicated
- grad_gate: bfloat16 [2048, 32, 768], P('dp', 'expert')
- grad_up: bfloat16 [2048, 32, 768], P('dp', 'expert')
- grad_down: bfloat16 [2048, 32, 768], P('dp', 'expert')
Inputs may be any that keep to these rules, and one draw needn't show every extreme that they name: The 40 picks of one expert on one device are distinct token positions of that device.
All inputs are finite; a program needn't handle non-finite values.
Results may differ from a plain program's by a relative error of at most 0.018.
Values may be sent and summed in bfloat16 or wider, within the bound.
A program may use at most 192 MiB of HBM per device.

v0:
```python
import math
import jax
import jax.numpy as jnp
from jax import lax
from jax.sharding import PartitionSpec as P

BF = jnp.bfloat16
F32 = jnp.float32


def body(tokens, probe, domain, mix, router, picks, w_gate, w_up, w_down):
    token_count, model_width = tokens.shape
    expert_count = router.shape[1]
    slot_count = picks.shape[2]
    pick_count = expert_count * slot_count
    domain_count = mix.shape[0]
    device_count = lax.axis_size("dp") * lax.axis_size("expert")
    flat = picks[0].reshape(pick_count)
    token_ids = jnp.arange(token_count, dtype=jnp.int32)
    select = (flat[:, None] == token_ids[None, :]).astype(BF)
    expert_of = jnp.repeat(jnp.arange(expert_count, dtype=jnp.int32), slot_count)
    own_expert = expert_of[:, None] == jnp.arange(expert_count, dtype=jnp.int32)[None, :]
    outgoing = jnp.dot(select, tokens, preferred_element_type=F32).astype(BF)
    received = lax.all_to_all(
        outgoing.reshape(expert_count, 1, slot_count, model_width),
        "expert",
        split_axis=0,
        concat_axis=1,
        tiled=True,
    )
    logits = jnp.dot(outgoing, router, preferred_element_type=F32)
    gate = jax.nn.sigmoid(jnp.sum(jnp.where(own_expert, logits, 0.0), axis=1))
    pre_gate = jnp.einsum("jsrd,djf->jsrf", received, w_gate, preferred_element_type=F32)
    pre_up = jnp.einsum("jsrd,djf->jsrf", received, w_up, preferred_element_type=F32)
    hidden = (jax.nn.silu(pre_gate) * pre_up).astype(BF)
    result = jnp.einsum("jsrf,djf->jsrd", hidden, w_down, preferred_element_type=F32).astype(BF)
    returned = lax.all_to_all(result, "expert", split_axis=1, concat_axis=0, tiled=True)
    returned = returned.reshape(pick_count, model_width)
    weighted = jnp.where(
        flat[None, :] == token_ids[:, None], gate.astype(BF)[None, :], jnp.zeros((), BF)
    )
    added = jnp.dot(weighted, returned, preferred_element_type=F32)
    difference = tokens.astype(F32) + added - probe.astype(F32)
    per_token = jnp.sum(difference * difference, axis=1)
    member = (domain[:, None] == jnp.arange(domain_count, dtype=jnp.int32)[None, :]).astype(F32)
    local_loss = jnp.sum(per_token[:, None] * member, axis=0)
    loss_scale = 1.0 / math.sqrt(device_count * slot_count)
    weight_tok = jnp.sum(member * mix[None, :], axis=1)
    upstream = ((loss_scale * weight_tok)[:, None] * difference).astype(BF)
    picked_up = jnp.dot(select, upstream, preferred_element_type=F32)
    sending = (gate[:, None] * picked_up).astype(BF)
    gate_slope = jnp.sum(picked_up * returned.astype(F32), axis=1)
    logit_grad = gate_slope * gate * (1.0 - gate)
    placing = jnp.where(own_expert, logit_grad[:, None], 0.0)
    high = placing.astype(BF)
    low = (placing - high.astype(F32)).astype(BF)
    placed = lax.dot_general(
        select,
        jnp.concatenate([high, low], axis=1),
        (((0,), (0,)), ((), ())),
        preferred_element_type=F32,
    ).astype(BF)
    router_part = lax.dot_general(
        tokens, placed, (((0,), (0,)), ((), ())), preferred_element_type=F32
    )
    router_part = router_part[:, :expert_count] + router_part[:, expert_count:]
    loss_rows = jnp.zeros((8, expert_count), F32).at[0, :domain_count].set(local_loss)
    summed = lax.psum(jnp.concatenate([router_part, loss_rows], axis=0), ("dp", "expert"))
    back_grad = lax.all_to_all(
        sending.reshape(expert_count, 1, slot_count, model_width),
        "expert",
        split_axis=0,
        concat_axis=1,
        tiled=True,
    )

    def reduced(left, right):
        part = jnp.einsum("jsrd,jsrf->djf", left, right, preferred_element_type=F32)
        return lax.psum_scatter(part.astype(BF), "dp", scatter_dimension=0, tiled=True)

    grad_down = reduced(back_grad, hidden)
    hidden_grad = jnp.einsum("jsrd,djf->jsrf", back_grad, w_down, preferred_element_type=F32)
    sigmoid_gate = jax.nn.sigmoid(pre_gate)
    gate_in = (
        hidden_grad * pre_up * sigmoid_gate * (1.0 + pre_gate * (1.0 - sigmoid_gate))
    ).astype(BF)
    up_in = (hidden_grad * (pre_gate * sigmoid_gate)).astype(BF)
    grad_gate = reduced(received, gate_in)
    grad_up = reduced(received, up_in)
    domain_loss = summed[model_width, :domain_count] * (
        domain_count / (token_count * device_count * model_width)
    )
    return (domain_loss, summed[:model_width], grad_gate, grad_up, grad_down)


def solution(mesh):
    placed = (
        P(("dp", "expert"), None),
        P(("dp", "expert"), None),
        P(("dp", "expert")),
        P(),
        P(),
        P(("dp", "expert"), None, None),
        P(None, "expert", None),
        P(None, "expert", None),
        P(None, "expert", None),
    )
    return jax.shard_map(
        body,
        mesh=mesh,
        in_specs=placed,
        out_specs=(
            P(),
            P(),
            P("dp", "expert", None),
            P("dp", "expert", None),
            P("dp", "expert", None),
        ),
        check_vma=False,
    )
```

profile of v0, /device:TPU:1, one launch (start us, length us, event | category | flops | bytes accessed | tf_op | source)
XLA Modules:
  0.0 530.8 jit_solution(12913081817586084446)
XLA Ops:
  8.0 0.0 copy-start
  8.0 0.8 eq.64
  8.9 4.9 convolution_convert_fusion
  13.8 0.0 copy-start.7
  13.8 0.0 slice-start
  13.8 71.2 %all_to_all.51 = bf16[32,1,40,2048]{3,2,1,0:T(8,128)(2,1)S(1)} all-to-all(bf16[32,1,40,2048]{3,2,1,0:T(8,128)(2,1)S(1)} %bitcast.69), channel_id=1, replica_groups=mesh['dp'=8,'expert'=16] {'expert'}, dimensions={0} | all-to-all | bytes 10485760 | tf_op jit(solution)/shard_map/all_to_all | solution.py:24
  85.0 4.4 fusion.5
  89.4 0.0 copy-start.8
  89.4 0.0 copy-done.3
  89.4 0.0 slice-done
  89.4 0.0 slice-done.1
  89.4 6.5 %multiply_convert_fusion.4 = (bf16[2,16,40,768]{3,2,1,0:T(8,128)(2,1)}, f32[2,16,40,768]{3,2,1,0:T(8,128)}) fusion(f32[2,16,40,768]{3,2,1,0:T(8,128)S(1)} %fusion.5, bf16[2048,2,768,1]{2,1,0,3:T(2,128)(2,1)S(1)} %bitcast.79, bf16[16,2,1,40,2048]{4,3,1,0,2:T(8,128)(2,1)S(1)} %bitcast.71), kind=kOutput, calls=%fused_computation.31 | convolution fusion | flops 4032430080 | bytes 21364736 | tf_op jit(solution)/shard_map/jsrd,djf->jsrf/dot_general | solution.py:34
  96.0 7.7 %fusion.19 = bf16[2,16,40,2048]{3,2,1,0:T(8,128)(2,1)S(1)} fusion(bf16[2,16,40,768]{3,2,1,0:T(8,128)(2,1)} %get-tuple-element.43, bf16[2048,2,768,1]{2,1,0,3:T(2,128)(2,1)} %bitcast.80), kind=kOutput, calls=%fused_computation.28 | convolution fusion | flops 4029153280 | bytes 13500416 | tf_op jit(solution)/shard_map/jsrf,djf->jsrd/dot_general | solution.py:36
  103.6 2.8 copy.51
  106.4 5.7 %all-to-all-start.1 = ((bf16[2,16,40,2048]{3,2,0,1:T(8,128)(2,1)}), bf16[2,16,40,2048]{3,2,0,1:T(8,128)(2,1)}, u32[]{:S(2)}, u32[]{:S(2)}) async-start(bf16[2,16,40,2048]{3,2,0,1:T(8,128)(2,1)} %copy.51), calls=%async_computation.1 | async-start | bytes 10485760 | tf_op jit(solution)/shard_map/all_to_all | solution.py:37
  112.2 0.1 eq.68
  112.2 4.3 fusion.38
  116.6 64.9 %all-to-all-done.1 = bf16[2,16,40,2048]{3,2,0,1:T(8,128)(2,1)} async-done(((bf16[2,16,40,2048]{3,2,0,1:T(8,128)(2,1)}), bf16[2,16,40,2048]{3,2,0,1:T(8,128)(2,1)}, u32[]{:S(2)}, u32[]{:S(2)}) %all-to-all-start.1) | async-done | bytes 5242912 | tf_op jit(solution)/shard_map/all_to_all | solution.py:37
  181.5 6.5 %multiply_reduce_fusion.1 = (f32[512]{0:T(512)S(1)}, f32[512,2048]{1,0:T(8,128)S(1)}) fusion(bf16[512,2048]{1,0:T(8,128)(2,1)} %param.12, bf16[1280,2048]{1,0:T(8,128)(2,1)} %bitcast.11, s32[1280]{0:T(1024)S(1)} %eq.64, bf16[1280]{0:T(1024)(128)(2,1)S(1)} %get-tuple-element.42, bf16[512,2048]{1,0:T(8,128)(2,1)S(1)} %copy-done.4), kind=kOutput, calls=%fused_computation.25 | convolution fusion | flops 2691956224 | bytes 13641216 | tf_op jit(solution)/shard_map/dot_general | solution.py:42
  188.0 0.1 select_reduce_fusion.1
  188.1 7.4 %multiply_convert_fusion = (bf16[1280,2048]{1,0:T(8,128)(2,1)}, f32[1280]{0:T(1024)S(1)}) fusion(f32[1280]{0:T(1024)S(1)} %get-tuple-element.41, bf16[2,16,40,2048]{3,2,0,1:T(8,128)(2,1)} %all-to-all-done.1, f32[512,2048]{1,0:T(8,128)S(1)} %get-tuple-element.46, f32[512]{0:T(512)S(1)} %broadcast_multiply_fusion, s32[1280]{0:T(1024)S(1)} %eq.64), kind=kOutput, calls=%fused_computation.3 | convolution fusion | flops 2700212992 | bytes 14697472 | tf_op jit(solution)/shard_map/dot_general | solution.py:50
  195.5 14.7 %all-to-all-start.2 = ((bf16[32,1,40,2048]{3,2,1,0:T(8,128)(2,1)}), bf16[32,1,40,2048]{3,2,1,0:T(8,128)(2,1)}, u32[]{:S(2)}, u32[]{:S(2)}) async-start(bf16[32,1,40,2048]{3,2,1,0:T(8,128)(2,1)} %bitcast.74), calls=%async_computation.2 | async-start | bytes 10485760 | tf_op jit(solution)/shard_map/all_to_all | solution.py:69
  210.2 0.0 all-reduce.3.cloned.1.call-start
  210.2 0.1 copy.52
  210.4 1.0 convolution_bitcast_fusion
  211.5 0.7 select_maximum_fusion
  212.2 0.0 all-reduce.3.cloned.1.call-update
  212.2 0.0 reduce-scatter.8.cloned.1.call-start
  212.3 68.4 %all-to-all-done.2 = bf16[32,1,40,2048]{3,2,1,0:T(8,128)(2,1)} async-done(((bf16[32,1,40,2048]{3,2,1,0:T(8,128)(2,1)}), bf16[32,1,40,2048]{3,2,1,0:T(8,128)(2,1)}, u32[]{:S(2)}, u32[]{:S(2)}) %all-to-all-start.2) | async-done | bytes 5242912 | tf_op jit(solution)/shard_map/all_to_all | solution.py:69
  280.7 9.8 %fusion.2 = bf16[2048,2,768]{0,2,1:T(8,128)(2,1)} fusion(bf16[2,16,40,768]{3,2,1,0:T(8,128)(2,1)} %get-tuple-element.43, bf16[16,2,1,40,2048]{4,3,1,0,2:T(8,128)(2,1)} %bitcast.18), kind=kOutput, calls=%fused_computation.8 | convolution fusion | flops 4029677568 | bytes 13500416 | tf_op jit(solution)/shard_map/jsrd,jsrf->djf/dot_general | solution.py:78
  290.5 0.0 reduce-scatter.8.cloned.1.call-update
  290.5 0.3 reduce-scatter.6.cloned.1.call-start
  290.8 8.2 %fusion.7 = f32[2,16,40,768]{3,2,1,0:T(8,128)S(1)} fusion(bf16[2048,2,768,1]{2,1,0,3:T(2,128)(2,1)} %bitcast.81, bf16[16,2,1,40,2048]{4,3,1,0,2:T(8,128)(2,1)} %bitcast.18), kind=kOutput, calls=%fused_computation.13 | convolution fusion | flops 4026531840 | bytes 15466496 | tf_op jit(solution)/shard_map/jsrd,djf->jsrf/dot_general | solution.py:82
  299.0 1.8 copy-done.10
  300.9 9.9 %fusion.1 = bf16[2048,2,768]{0,2,1:T(8,128)(2,1)} fusion(bf16[16,2,1,40,2048]{4,3,1,0,2:T(8,128)(2,1)} %bitcast.72, f32[2,16,40,768]{3,2,1,0:T(8,128)S(1)} %fusion.7, f32[2,16,40,768]{3,2,1,0:T(8,128)S(1)} %copy-done.9), kind=kOutput, calls=%fused_computation.7 | convolution fusion | flops 4035575808 | bytes 19398656 | tf_op jit(solution)/shard_map/jsrd,jsrf->djf/dot_general | solution.py:78
  310.8 0.0 reduce-scatter.6.cloned.1.call-update
  310.8 0.0 reduce-scatter.4.cloned.1.call-start
  310.8 12.3 %fusion = bf16[2048,2,768]{0,2,1:T(8,128)(2,1)} fusion(bf16[16,2,1,40,2048]{4,3,1,0,2:T(8,128)(2,1)} %bitcast.73, f32[2,16,40,768]{3,2,1,0:T(8,128)} %copy-done.8, f32[2,16,40,768]{3,2,1,0:T(8,128)} %copy-done.10, f32[2,16,40,768]{3,2,1,0:T(8,128)} %get-tuple-element.44), kind=kOutput, calls=%fused_computation.6 | convolution fusion | flops 4039507968 | bytes 23330816 | tf_op jit(solution)/shard_map/jsrd,jsrf->djf/dot_general | solution.py:78
  323.1 0.0 reduce-scatter.4.cloned.1.call-update
  323.1 0.0 copy-start.1
  323.2 129.6 %all-reduce.3.cloned.1.call-done = f32[2056,32]{0,1:T(8,128)} async-done(((f32[2056,32]{0,1:T(8,128)}), f32[2056,32]{0,1:T(8,128)}) %all-reduce.3.cloned.1.call-update) | async-done | bytes 263184 | tf_op jit(solution)/shard_map/psum | solution.py:68
  452.8 1.7 slice.35
  454.4 1.3 fusion.49
  455.8 3.1 copy.58
  458.9 3.0 copy.57
  461.9 58.3 %reduce-scatter.4.cloned.1.call-done = bf16[256,2,768]{0,2,1:T(8,128)(2,1)} async-done(((bf16[2048,2,768]{0,2,1:T(8,128)(2,1)}), bf16[256,2,768]{0,2,1:T(8,128)(2,1)}) %reduce-scatter.4.cloned.1.call-update) | async-done | bytes 786448 | tf_op jit(solution)/shard_map/reduce_scatter | solution.py:79
  520.2 3.0 copy.56
  523.3 0.0 copy-done.1
  (26 shorter events, 0.1 us)
Async XLA Ops:
  8.0 104.2 %copy-start = (bf16[2048,32]{0,1:T(8,128)(2,1)S(1)}, bf16[2048,32]{0,1:T(8,128)(2,1)}, u32[]{:S(2)}) copy-start(bf16[2048,32]{0,1:T(8,128)(2,1)} %param.15) | copy-start | bytes 393220
  13.8 71.2 %copy-start.2 = (bf16[1280,2048]{1,0:T(8,128)(2,1)}, bf16[1280,2048]{1,0:T(8,128)(2,1)S(1)}, u32[]{:S(2)}) copy-start(bf16[1280,2048]{1,0:T(8,128)(2,1)S(1)} %convolution_convert_fusion) | copy-start | bytes 15728644
  13.8 71.2 %copy-start.7 = (bf16[2048,2,768]{2,1,0:T(2,128)(2,1)S(1)}, bf16[2048,2,768]{2,1,0:T(2,128)(2,1)}, u32[]{:S(2)}) copy-start(bf16[2048,2,768]{2,1,0:T(2,128)(2,1)} %param.17) | copy-start | bytes 18874372
  13.8 75.6 %slice-start = ((s8[6291456]{0:T(1024)(128)(4,1)}), s8[4194304]{0:T(1024)(128)(4,1)S(1)}, s32[]{:S(2)}) async-start(s8[6291456]{0:T(1024)(128)(4,1)} %bitcast.77), calls=%async_computation.10 | async-start | bytes 8388608
  85.0 4.4 copy-start.3
  85.0 4.4 slice-start.1
  89.4 6.6 %copy-start.8 = (f32[2,16,40,768]{3,2,1,0:T(8,128)}, f32[2,16,40,768]{3,2,1,0:T(8,128)S(1)}, u32[]{:S(2)}) copy-start(f32[2,16,40,768]{3,2,1,0:T(8,128)S(1)} %fusion.5) | copy-start | bytes 11796484
  106.4 75.0 %all-to-all-start.1 = ((bf16[2,16,40,2048]{3,2,0,1:T(8,128)(2,1)}), bf16[2,16,40,2048]{3,2,0,1:T(8,128)(2,1)}, u32[]{:S(2)}, u32[]{:S(2)}) async-start(bf16[2,16,40,2048]{3,2,0,1:T(8,128)(2,1)} %copy.51), calls=%async_computation.1 | async-start | bytes 10485760 | tf_op jit(solution)/shard_map/all_to_all | solution.py:37
  112.1 69.3 %copy-start.4 = (bf16[512,2048]{1,0:T(8,128)(2,1)S(1)}, bf16[512,2048]{1,0:T(8,128)(2,1)}, u32[]{:S(2)}) copy-start(bf16[512,2048]{1,0:T(8,128)(2,1)} %param.11) | copy-start | bytes 6291460
  181.5 6.5 %copy-start.5 = (s32[512]{0:T(512)S(1)}, s32[512]{0:T(512)}, u32[]{:S(2)}) copy-start(s32[512]{0:T(512)} %param.13) | copy-start | bytes 6148
  181.5 6.5 %copy-start.6 = (f32[22]{0:T(128)S(1)}, f32[22]{0:T(128)}, u32[]{:S(2)}) copy-start(f32[22]{0:T(128)} %param.14) | copy-start | bytes 268
  195.5 85.2 %all-to-all-start.2 = ((bf16[32,1,40,2048]{3,2,1,0:T(8,128)(2,1)}), bf16[32,1,40,2048]{3,2,1,0:T(8,128)(2,1)}, u32[]{:S(2)}, u32[]{:S(2)}) async-start(bf16[32,1,40,2048]{3,2,1,0:T(8,128)(2,1)} %bitcast.74), calls=%async_computation.2 | async-start | bytes 10485760 | tf_op jit(solution)/shard_map/all_to_all | solution.py:69
  210.2 242.6 %all-reduce.3.cloned.1.call-start = ((), (), s32[]{:S(2)}) async-start(), calls=%async_computation.6 | async-start | bytes 557056 | tf_op jit(solution)/shard_map/psum | solution.py:68
  212.2 243.5 %reduce-scatter.8.cloned.1.call-start = ((), (), s32[]{:S(2)}) async-start(), calls=%async_computation.9 | async-start | bytes 7077888 | tf_op jit(solution)/shard_map/reduce_scatter | solution.py:79
  290.5 168.3 %reduce-scatter.6.cloned.1.call-start = ((), (), s32[]{:S(2)}) async-start(), calls=%async_computation.8 | async-start | bytes 7077888 | tf_op jit(solution)/shard_map/reduce_scatter | solution.py:79
  290.8 10.1 %copy-start.9 = (f32[2,16,40,768]{3,2,1,0:T(8,128)S(1)}, f32[2,16,40,768]{3,2,1,0:T(8,128)}, u32[]{:S(2)}) copy-start(f32[2,16,40,768]{3,2,1,0:T(8,128)} %copy-done.8) | copy-start | bytes 11796484
  299.0 1.9 copy-start.10
  310.8 209.4 %reduce-scatter.4.cloned.1.call-start = ((), (), s32[]{:S(2)}) async-start(), calls=%async_computation.7 | async-start | bytes 7077888 | tf_op jit(solution)/shard_map/reduce_scatter | solution.py:79
  323.1 200.1 %copy-start.1 = (bf16[2048,32]{0,1:T(8,128)(2,1)S(1)}, bf16[2048,32]{0,1:T(8,128)(2,1)}, u32[]{:S(2)}) copy-start(bf16[2048,32]{0,1:T(8,128)(2,1)} %param.15) | copy-start | bytes 393220
Sparse Core Ops, SparseCore 0:
  216.3 236.3 all-reduce.2
Sparse Core Ops, SparseCore 1:
  290.6 81.2 reduce-scatter.7
  374.2 71.8 reduce-scatter.5
  448.3 71.9 reduce-scatter.3
where the time goes:
time: 531 us
  waiting for transfers between devices  321 us (60%)
  matrix products  82.8 us (16%)
  blocking collectives  71.2 us (13%)
  starting transfers between devices  20.8 us (4%)
  local copies, waits for them, and re-layouts  16.6 us (3%)
  between operations  15.9 us (3%)
    psum x1, waiting for transfers between devices, body(): lax.psum(jnp.concatenate([router_part, loss_rows], axis=0), ('dp', 'exper...  130 us
    all_to_all x1, blocking collectives, body(): lax.all_to_all(outgoing.reshape(expert_count, 1, slot_count, model_width)...  71.2 us
    all_to_all x1, waiting for transfers between devices, body(): lax.all_to_all(sending.reshape(expert_count, 1, slot_count, model_width),...  68.4 us
    all_to_all x1, waiting for transfers between devices, body(): lax.all_to_all(result, 'expert', split_axis=1, concat_axis=0, tiled=True)  64.9 us
    reduce_scatter x3, waiting for transfers between devices, reduced(): lax.psum_scatter(part.astype(BF), 'dp', scatter_dimension=0, tiled=True)  58.3 us
    dot_general x3, matrix products, reduced(): part = jnp.einsum('jsrd,jsrf->djf', left, right, preferred_element_type=F32)  32 us
    all_to_all x1, starting transfers between devices, body(): lax.all_to_all(sending.reshape(expert_count, 1, slot_count, model_width),...  14.7 us
    unnamed x29, local copies, waits for them, and re-layouts  11.1 us
  transfers between devices with their start and end apart: 6, of which 4 were waited for; matrix products, arithmetic and copies ran while one was open for 10% of the time, Pallas kernels for 0%

commit v1 on v0

--- a/solution.py
+++ b/solution.py
@@ -65,7 +65,9 @@
     )
     router_part = router_part[:, :expert_count] + router_part[:, expert_count:]
     loss_rows = jnp.zeros((8, expert_count), F32).at[0, :domain_count].set(local_loss)
-    summed = lax.psum(jnp.concatenate([router_part, loss_rows], axis=0), ("dp", "expert"))
+    summed = jnp.concatenate([router_part, loss_rows], axis=0)
+    for axis in ("dp", "expert"):
+        summed = lax.psum(summed, axis)
     back_grad = lax.all_to_all(
         sending.reshape(expert_count, 1, slot_count, model_width),
         "expert",

time: 531 us -> 658 us (1.24)
  waiting for transfers between devices: 321 us -> 450 us
    reduce_scatter x3, waiting for transfers between devices: 58.3 us -> 217 us  [reduced(): lax.psum_scatter(part.astype(BF), 'dp', scatter_dimension=0, tiled=True)]
    all_to_all x1, waiting for transfers between devices: 68.4 us -> 0.01 us  [body(): lax.all_to_all(sending.reshape(expert_count, 1, slot_count, model_width),...]
    psum x1 -> x2, waiting for transfers between devices: 130 us -> 168 us  [body(): summed = lax.psum(summed, axis)]
  transfers between devices with their start and end apart: 6 -> 7, of which waited for: 4 -> 6; matrix products, arithmetic and copies ran while one was open for 10% -> 8% of each run, Pallas kernels for 0% -> 0%
where the time goes in v1:
time: 658 us; the launch traced here: 657 us
  waiting for transfers between devices  450 us (68%)
  matrix products  82.8 us (13%)
  blocking collectives  71.2 us (11%)
  starting transfers between devices  20.8 us (3%)
  local copies, waits for them, and re-layouts  16.5 us (3%)
  between operations  14 us (2%)
    reduce_scatter x3, waiting for transfers between devices, reduced(): lax.psum_scatter(part.astype(BF), 'dp', scatter_dimension=0, tiled=True)  217 us
    psum x2, waiting for transfers between devices, body(): summed = lax.psum(summed, axis)  168 us
    all_to_all x1, blocking collectives, body(): lax.all_to_all(outgoing.reshape(expert_count, 1, slot_count, model_width)...  71.2 us
    all_to_all x1, waiting for transfers between devices, body(): lax.all_to_all(result, 'expert', split_axis=1, concat_axis=0, tiled=True)  64.9 us
    dot_general x3, matrix products, reduced(): part = jnp.einsum('jsrd,jsrf->djf', left, right, preferred_element_type=F32)  32 us
    all_to_all x1, starting transfers between devices, body(): lax.all_to_all(sending.reshape(expert_count, 1, slot_count, model_width),...  14.7 us
  transfers between devices with their start and end apart: 7, of which 6 were waited for; matrix products, arithmetic and copies ran while one was open for 8% of the time, Pallas kernels for 0%

profile of v1, /device:TPU:1, one launch (start us, length us, event | category | flops | bytes accessed | tf_op | source)
XLA Modules:
  0.0 657.3 jit_solution(14622293042635914174)
XLA Ops:
  7.2 0.0 copy-start
  7.2 0.8 eq.64
  8.0 4.9 convolution_convert_fusion
  13.0 0.0 copy-start.7
  13.0 0.0 slice-start
  13.0 71.2 %all_to_all.51 = bf16[32,1,40,2048]{3,2,1,0:T(8,128)(2,1)S(1)} all-to-all(bf16[32,1,40,2048]{3,2,1,0:T(8,128)(2,1)S(1)} %bitcast.69), channel_id=1, replica_groups=mesh['dp'=8,'expert'=16] {'expert'}, dimensions={0} | all-to-all | bytes 10485760 | tf_op jit(solution)/shard_map/all_to_all | solution.py:24
  84.2 4.4 fusion.5
  88.6 6.5 multiply_convert_fusion.4
  95.1 7.7 %fusion.19 = bf16[2,16,40,2048]{3,2,1,0:T(8,128)(2,1)S(1)} fusion(bf16[2,16,40,768]{3,2,1,0:T(8,128)(2,1)} %get-tuple-element.43, bf16[2048,2,768,1]{2,1,0,3:T(2,128)(2,1)} %bitcast.80), kind=kOutput, calls=%fused_computation.28 | convolution fusion | flops 4029153280 | bytes 13500416 | tf_op jit(solution)/shard_map/jsrf,djf->jsrd/dot_general | solution.py:36
  102.8 2.8 copy.51
  105.6 5.7 all-to-all-start.1
  111.3 0.1 eq.68
  111.4 4.3 fusion.38
  115.7 64.9 %all-to-all-done.1 = bf16[2,16,40,2048]{3,2,0,1:T(8,128)(2,1)} async-done(((bf16[2,16,40,2048]{3,2,0,1:T(8,128)(2,1)}), bf16[2,16,40,2048]{3,2,0,1:T(8,128)(2,1)}, u32[]{:S(2)}, u32[]{:S(2)}) %all-to-all-start.1) | async-done | bytes 5242912 | tf_op jit(solution)/shard_map/all_to_all | solution.py:37
  180.6 6.5 multiply_reduce_fusion.1
  187.1 0.1 select_reduce_fusion.1
  187.3 7.4 %multiply_convert_fusion = (bf16[1280,2048]{1,0:T(8,128)(2,1)}, f32[1280]{0:T(1024)S(1)}) fusion(f32[1280]{0:T(1024)S(1)} %get-tuple-element.41, bf16[2,16,40,2048]{3,2,0,1:T(8,128)(2,1)} %all-to-all-done.1, f32[512,2048]{1,0:T(8,128)S(1)} %get-tuple-element.46, f32[512]{0:T(512)S(1)} %broadcast_multiply_fusion, s32[1280]{0:T(1024)S(1)} %eq.64), kind=kOutput, calls=%fused_computation.3 | convolution fusion | flops 2700212992 | bytes 14697472 | tf_op jit(solution)/shard_map/dot_general | solution.py:50
  194.6 14.7 %all-to-all-start.2 = ((bf16[32,1,40,2048]{3,2,1,0:T(8,128)(2,1)}), bf16[32,1,40,2048]{3,2,1,0:T(8,128)(2,1)}, u32[]{:S(2)}, u32[]{:S(2)}) async-start(bf16[32,1,40,2048]{3,2,1,0:T(8,128)(2,1)} %bitcast.74), calls=%async_computation.2 | async-start | bytes 10485760 | tf_op jit(solution)/shard_map/all_to_all | solution.py:71
  209.3 0.0 all-reduce.4.cloned.1.call-start
  209.4 0.1 copy.52
  209.6 1.0 convolution_bitcast_fusion
  210.6 0.7 select_maximum_fusion
  211.4 0.0 all-reduce.4.cloned.1.call-update
  211.4 0.0 all-reduce.6.cloned.1.call-start
  211.4 73.4 %all-reduce.4.cloned.1.call-done = f32[2056,32]{0,1:T(8,128)} async-done(((f32[2056,32]{0,1:T(8,128)}), f32[2056,32]{0,1:T(8,128)}) %all-reduce.4.cloned.1.call-update) | async-done | bytes 263184 | tf_op jit(solution)/shard_map/psum | solution.py:70
  284.8 0.0 all-reduce.6.cloned.1.call-update
  284.8 0.0 reduce-scatter.8.cloned.1.call-start
  284.9 0.0 all-to-all-done.2
  284.9 9.8 %fusion.2 = bf16[2048,2,768]{0,2,1:T(8,128)(2,1)} fusion(bf16[2,16,40,768]{3,2,1,0:T(8,128)(2,1)} %get-tuple-element.43, bf16[16,2,1,40,2048]{4,3,1,0,2:T(8,128)(2,1)} %bitcast.18), kind=kOutput, calls=%fused_computation.8 | convolution fusion | flops 4029677568 | bytes 13500416 | tf_op jit(solution)/shard_map/jsrd,jsrf->djf/dot_general | solution.py:80
  294.7 0.0 reduce-scatter.8.cloned.1.call-update
  294.7 0.3 reduce-scatter.6.cloned.1.call-start
  295.0 8.2 %fusion.7 = f32[2,16,40,768]{3,2,1,0:T(8,128)S(1)} fusion(bf16[2048,2,768,1]{2,1,0,3:T(2,128)(2,1)} %bitcast.81, bf16[16,2,1,40,2048]{4,3,1,0,2:T(8,128)(2,1)} %bitcast.18), kind=kOutput, calls=%fused_computation.13 | convolution fusion | flops 4026531840 | bytes 15466496 | tf_op jit(solution)/shard_map/jsrd,djf->jsrf/dot_general | solution.py:84
  303.2 1.8 copy-done.10
  305.1 9.9 %fusion.1 = bf16[2048,2,768]{0,2,1:T(8,128)(2,1)} fusion(bf16[16,2,1,40,2048]{4,3,1,0,2:T(8,128)(2,1)} %bitcast.72, f32[2,16,40,768]{3,2,1,0:T(8,128)S(1)} %fusion.7, f32[2,16,40,768]{3,2,1,0:T(8,128)S(1)} %copy-done.9), kind=kOutput, calls=%fused_computation.7 | convolution fusion | flops 4035575808 | bytes 19398656 | tf_op jit(solution)/shard_map/jsrd,jsrf->djf/dot_general | solution.py:80
  314.9 0.0 reduce-scatter.6.cloned.1.call-update
  315.0 0.0 reduce-scatter.4.cloned.1.call-start
  315.0 12.3 %fusion = bf16[2048,2,768]{0,2,1:T(8,128)(2,1)} fusion(bf16[16,2,1,40,2048]{4,3,1,0,2:T(8,128)(2,1)} %bitcast.73, f32[2,16,40,768]{3,2,1,0:T(8,128)} %copy-done.8, f32[2,16,40,768]{3,2,1,0:T(8,128)} %copy-done.10, f32[2,16,40,768]{3,2,1,0:T(8,128)} %get-tuple-element.44), kind=kOutput, calls=%fused_computation.6 | convolution fusion | flops 4039507968 | bytes 23330816 | tf_op jit(solution)/shard_map/jsrd,jsrf->djf/dot_general | solution.py:80
  327.3 0.0 reduce-scatter.4.cloned.1.call-update
  327.3 0.0 copy-start.1
  327.3 94.8 %all-reduce.6.cloned.1.call-done = f32[2056,32]{0,1:T(8,128)} async-done(((f32[2056,32]{0,1:T(8,128)}), f32[2056,32]{0,1:T(8,128)}) %all-reduce.6.cloned.1.call-update) | async-done | bytes 263184 | tf_op jit(solution)/shard_map/psum | solution.py:70
  422.1 1.7 slice.35
  423.8 1.3 fusion.49
  425.1 74.6 %reduce-scatter.8.cloned.1.call-done = bf16[256,2,768]{0,2,1:T(8,128)(2,1)} async-done(((bf16[2048,2,768]{0,2,1:T(8,128)(2,1)}), bf16[256,2,768]{0,2,1:T(8,128)(2,1)}) %reduce-scatter.8.cloned.1.call-update) | async-done | bytes 786448 | tf_op jit(solution)/shard_map/reduce_scatter | solution.py:81
  499.7 3.0 copy.58
  502.8 71.0 %reduce-scatter.6.cloned.1.call-done = bf16[256,2,768]{0,2,1:T(8,128)(2,1)} async-done(((bf16[2048,2,768]{0,2,1:T(8,128)(2,1)}), bf16[256,2,768]{0,2,1:T(8,128)(2,1)}) %reduce-scatter.6.cloned.1.call-update) | async-done | bytes 786448 | tf_op jit(solution)/shard_map/reduce_scatter | solution.py:81
  573.7 3.0 copy.57
  576.8 70.9 %reduce-scatter.4.cloned.1.call-done = bf16[256,2,768]{0,2,1:T(8,128)(2,1)} async-done(((bf16[2048,2,768]{0,2,1:T(8,128)(2,1)}), bf16[256,2,768]{0,2,1:T(8,128)(2,1)}) %reduce-scatter.4.cloned.1.call-update) | async-done | bytes 786448 | tf_op jit(solution)/shard_map/reduce_scatter | solution.py:81
  647.7 3.0 copy.56
  (29 shorter events, 0.1 us)
Async XLA Ops:
  7.2 104.2 %copy-start = (bf16[2048,32]{0,1:T(8,128)(2,1)S(1)}, bf16[2048,32]{0,1:T(8,128)(2,1)}, u32[]{:S(2)}) copy-start(bf16[2048,32]{0,1:T(8,128)(2,1)} %param.15) | copy-start | bytes 393220
  12.9 71.2 %copy-start.2 = (bf16[1280,2048]{1,0:T(8,128)(2,1)}, bf16[1280,2048]{1,0:T(8,128)(2,1)S(1)}, u32[]{:S(2)}) copy-start(bf16[1280,2048]{1,0:T(8,128)(2,1)S(1)} %convolution_convert_fusion) | copy-start | bytes 15728644
  13.0 71.2 %copy-start.7 = (bf16[2048,2,768]{2,1,0:T(2,128)(2,1)S(1)}, bf16[2048,2,768]{2,1,0:T(2,128)(2,1)}, u32[]{:S(2)}) copy-start(bf16[2048,2,768]{2,1,0:T(2,128)(2,1)} %param.17) | copy-start | bytes 18874372
  13.0 75.6 %slice-start = ((s8[6291456]{0:T(1024)(128)(4,1)}), s8[4194304]{0:T(1024)(128)(4,1)S(1)}, s32[]{:S(2)}) async-start(s8[6291456]{0:T(1024)(128)(4,1)} %bitcast.77), calls=%async_computation.11 | async-start | bytes 8388608
  84.2 4.4 copy-start.3
  84.2 4.4 slice-start.1
  88.6 6.6 copy-start.8
  105.6 75.0 %all-to-all-start.1 = ((bf16[2,16,40,2048]{3,2,0,1:T(8,128)(2,1)}), bf16[2,16,40,2048]{3,2,0,1:T(8,128)(2,1)}, u32[]{:S(2)}, u32[]{:S(2)}) async-start(bf16[2,16,40,2048]{3,2,0,1:T(8,128)(2,1)} %copy.51), calls=%async_computation.1 | async-start | bytes 10485760 | tf_op jit(solution)/shard_map/all_to_all | solution.py:37
  111.3 69.3 %copy-start.4 = (bf16[512,2048]{1,0:T(8,128)(2,1)S(1)}, bf16[512,2048]{1,0:T(8,128)(2,1)}, u32[]{:S(2)}) copy-start(bf16[512,2048]{1,0:T(8,128)(2,1)} %param.11) | copy-start | bytes 6291460
  180.6 6.5 copy-start.5
  180.6 6.5 copy-start.6
  194.6 90.3 %all-to-all-start.2 = ((bf16[32,1,40,2048]{3,2,1,0:T(8,128)(2,1)}), bf16[32,1,40,2048]{3,2,1,0:T(8,128)(2,1)}, u32[]{:S(2)}, u32[]{:S(2)}) async-start(bf16[32,1,40,2048]{3,2,1,0:T(8,128)(2,1)} %bitcast.74), calls=%async_computation.2 | async-start | bytes 10485760 | tf_op jit(solution)/shard_map/all_to_all | solution.py:71
  209.3 75.5 %all-reduce.4.cloned.1.call-start = ((), (), s32[]{:S(2)}) async-start(), calls=%async_computation.6 | async-start | bytes 557056 | tf_op jit(solution)/shard_map/psum | solution.py:70
  211.4 210.7 %all-reduce.6.cloned.1.call-start = ((), (), s32[]{:S(2)}) async-start(), calls=%async_computation.7 | async-start | bytes 557056 | tf_op jit(solution)/shard_map/psum | solution.py:70
  284.8 214.9 %reduce-scatter.8.cloned.1.call-start = ((), (), s32[]{:S(2)}) async-start(), calls=%async_computation.10 | async-start | bytes 7077888 | tf_op jit(solution)/shard_map/reduce_scatter | solution.py:81
  294.7 279.0 %reduce-scatter.6.cloned.1.call-start = ((), (), s32[]{:S(2)}) async-start(), calls=%async_computation.9 | async-start | bytes 7077888 | tf_op jit(solution)/shard_map/reduce_scatter | solution.py:81
  295.0 10.1 %copy-start.9 = (f32[2,16,40,768]{3,2,1,0:T(8,128)S(1)}, f32[2,16,40,768]{3,2,1,0:T(8,128)}, u32[]{:S(2)}) copy-start(f32[2,16,40,768]{3,2,1,0:T(8,128)} %copy-done.8) | copy-start | bytes 11796484
  303.2 1.9 copy-start.10
  315.0 332.7 %reduce-scatter.4.cloned.1.call-start = ((), (), s32[]{:S(2)}) async-start(), calls=%async_computation.8 | async-start | bytes 7077888 | tf_op jit(solution)/shard_map/reduce_scatter | solution.py:81
  327.3 323.4 %copy-start.1 = (bf16[2048,32]{0,1:T(8,128)(2,1)S(1)}, bf16[2048,32]{0,1:T(8,128)(2,1)}, u32[]{:S(2)}) copy-start(bf16[2048,32]{0,1:T(8,128)(2,1)} %param.15) | copy-start | bytes 393220
Sparse Core Ops, SparseCore 0:
  213.2 71.5 all-reduce.3
  287.5 134.6 all-reduce.5
  424.5 75.1 reduce-scatter.7
  502.0 71.6 reduce-scatter.5
  576.0 71.6 reduce-scatter.3
